TPU v7x, 128 devices: a whole 4x4x4 slice. The times are simulated.
128 devices in a mesh: row: 8 (over z, core), col: 16 (over y, x).
Axes of the slice: x: 4, y: 4, z: 4, core: 2. Of those that a mesh axis runs over, the one named last changes fastest.
Arguments:
- front_matrix: float32 [16384, 16384], P('row', 'col'), may hold values from -6 to 6
- child_tiles: float32 [8, 16, 16, 256, 256], P('row', 'col'), may hold values from -6 to 6
- target_column: int32 [8, 16, 16, 1], P('row', 'col'), may hold values from 0 to 15; in each aligned block of 16 rows (0 to 15, 16 to 31, ..., all dimensions but the last counted through in order) at most 2 rows name the same one
- target_tile: int32 [8, 16, 16], P('row', 'col'), may hold values from 0 to 31
- row_map: int32 [8, 16, 16, 256], P('row', 'col'), may hold values from 0 to 255, each once within a row
- col_map: int32 [8, 16, 16, 256], P('row', 'col'), may hold values from 0 to 255, each once within a row
- pivot_inverse: float32 [2, 256, 256], replicated, may hold values from -0.025 to 0.15
Outputs:
- front_out: float32 [16384, 16384], P('row', 'col')
Inputs may be any that keep to these rules, and one draw needn't show every extreme that they name: `target_column`: each device sends at most 2 of its tiles to one device column, and some device sends exactly 2 to one column.
All inputs are finite; a program needn't handle non-finite values.
Results may differ from a plain program's by a relative error of at most 0.0003.
Values sent between devices are 32-bit elements; how exact they have to be, the bound alone decides.
A program may use at most 128 MiB of HBM per device.

v0:
```python
import jax
import jax.numpy as jnp
from jax import lax
from jax.sharding import PartitionSpec as P

PANELS = 2
CAP = 2


highest_precision = lax.Precision.HIGHEST


def broadcast(array, axis, root):
    mine = lax.axis_index(axis) == root
    return lax.psum(jnp.where(mine, array, jnp.zeros_like(array)), axis)


def prepare(column, band_rows, inverse):
    lower = jnp.dot(column, inverse, precision=highest_precision)
    left_factor = broadcast(lower, "col", 0)
    right_factor = broadcast(band_rows, "row", 0)
    return (left_factor, right_factor, lower)


def live_masks(front_matrix, finish, row_start, col_start):
    row_live = row_start + jnp.arange(front_matrix.shape[0], dtype=jnp.int32) >= finish
    col_live = col_start + jnp.arange(front_matrix.shape[1], dtype=jnp.int32) >= finish
    return (row_live, col_live)


def eliminate(front_matrix, factors, panel_index, tile_size, row_start, col_start, first_column):
    left_factor, right_factor, lower = factors
    begin = panel_index * tile_size
    finish = begin + tile_size
    row_live, col_live = live_masks(front_matrix, finish, row_start, col_start)
    update = jnp.dot(left_factor, right_factor, precision=highest_precision)
    front_matrix = jnp.where(
        row_live[:, None] & col_live[None, :], front_matrix - update, front_matrix
    )
    strip = front_matrix[:, begin:finish]
    strip = jnp.where(row_live[:, None] & first_column, lower, strip)
    return front_matrix.at[:, begin:finish].set(strip)


def per_device(
    front_matrix, child_tiles, target_column, target_tile, row_map, col_map, pivot_inverse
):
    tile_size = child_tiles.shape[-1]
    tile_count = child_tiles.shape[2]
    col_total = lax.axis_size("col")
    slot_count = col_total * CAP
    outgoing = child_tiles.reshape(tile_count, tile_size, tile_size)
    targets = target_column.reshape(tile_count)
    order_ids = jnp.arange(tile_count, dtype=jnp.int32)
    before = (targets[:, None] == targets[None, :]) & (order_ids[None, :] < order_ids[:, None])
    placed = targets * CAP + jnp.sum(before.astype(jnp.int32), axis=1)
    index_maps = jnp.concatenate(
        [row_map.reshape(tile_count, tile_size), col_map.reshape(tile_count, tile_size)], axis=1
    ).astype(jnp.float32)
    sent_tiles = jnp.zeros((slot_count, tile_size, tile_size), jnp.float32).at[placed].set(outgoing)
    sent_maps = jnp.full((slot_count, 2 * tile_size), -1.0, jnp.float32).at[placed].set(index_maps)
    sent_index = (
        jnp.full((slot_count,), -1.0, jnp.float32)
        .at[placed]
        .set(target_tile.reshape(tile_count).astype(jnp.float32))
    )
    got_tiles, got_maps, got_index = (
        lax.all_to_all(
            sent_tiles.reshape(col_total, CAP, tile_size, tile_size),
            "col",
            split_axis=0,
            concat_axis=0,
            tiled=True,
        ),
        lax.all_to_all(
            sent_maps.reshape(col_total, CAP, 2 * tile_size),
            "col",
            split_axis=0,
            concat_axis=0,
            tiled=True,
        ),
        lax.all_to_all(
            sent_index.reshape(col_total, CAP), "col", split_axis=0, concat_axis=0, tiled=True
        ),
    )
    got_tiles = got_tiles.reshape(slot_count, tile_size, tile_size)
    got_maps = got_maps.reshape(slot_count, 2 * tile_size).astype(jnp.int32)
    local_tile = got_index.reshape(slot_count).astype(jnp.int32)
    is_valid = local_tile >= 0
    tile_rows = front_matrix.shape[0] // tile_size
    tile_cols = front_matrix.shape[1] // tile_size
    positions = jnp.arange(tile_size, dtype=jnp.int32)
    row_onehot = (
        (got_maps[:, None, :tile_size] == positions[None, :, None]) & is_valid[:, None, None]
    ).astype(jnp.float32)
    col_onehot = (got_maps[:, None, tile_size:] == positions[None, :, None]).astype(jnp.float32)
    permuted = jnp.einsum("sai,sij->saj", row_onehot, got_tiles, precision=highest_precision)
    arranged = jnp.einsum("saj,sbj->sab", permuted, col_onehot, precision=highest_precision)
    tile_ids = jnp.arange(tile_rows * tile_cols, dtype=jnp.int32)
    tile_onehot = (local_tile[:, None] == tile_ids[None, :]).astype(jnp.float32)
    summed = jnp.einsum("sk,sab->kab", tile_onehot, arranged, precision=highest_precision)
    summed = summed.reshape(tile_rows, tile_cols, tile_size, tile_size).transpose(0, 2, 1, 3)
    front_matrix = front_matrix + summed.reshape(front_matrix.shape)
    row_start = lax.axis_index("row") * front_matrix.shape[0]
    col_start = lax.axis_index("col") * front_matrix.shape[1]
    first_column = lax.axis_index("col") == 0
    for panel_index in range(PANELS):
        begin = panel_index * tile_size
        factors = prepare(
            front_matrix[:, begin : begin + tile_size],
            front_matrix[begin : begin + tile_size, :],
            pivot_inverse[panel_index],
        )
        front_matrix = eliminate(
            front_matrix, factors, panel_index, tile_size, row_start, col_start, first_column
        )
    return front_matrix


def solution(mesh):
    in_specs = (
        P("row", "col"),
        P("row", "col", None, None, None),
        P("row", "col", None, None),
        P("row", "col", None),
        P("row", "col", None, None),
        P("row", "col", None, None),
        P(),
    )
    out_specs = P("row", "col")
    return jax.shard_map(
        per_device, mesh=mesh, in_specs=in_specs, out_specs=out_specs, check_vma=False
    )
```

profile of v0, /device:TPU:12, one launch (start us, length us, event | category | flops | bytes accessed | tf_op | source)
XLA Modules:
  0.0 588.4 jit_solution(11801518623792215665)
XLA Ops:
  6.5 0.9 convert_reduce_fusion.1
  7.4 0.7 fusion.31
  8.1 0.7 convert_bitcast_fusion
  8.8 0.6 scatter_custom_fusion
  9.4 0.7 all_to_all.12
  10.1 7.3 %all-to-all-start = ((f32[16,1,2]{2,1,0:T(1,128)}), f32[16,1,2]{2,1,0:T(1,128)S(1)}, u32[]{:S(2)}, u32[]{:S(2)}) async-start(f32[16,1,2]{2,1,0:T(1,128)} %bitcast.5), calls=%async_computation | async-start | bytes 16384 | tf_op jit(solution)/shard_map/all_to_all | solution.py:82
  17.4 0.9 scatter_custom_fusion.1
  18.3 0.7 reshape.155
  19.0 2.8 all-to-all-done
  21.8 6.6 %all-to-all-start.1 = ((f32[16,2,512]{2,1,0:T(2,128)}), f32[16,2,512]{2,1,0:T(2,128)S(1)}, u32[]{:S(2)}, u32[]{:S(2)}) async-start(f32[16,2,512]{2,1,0:T(2,128)} %reshape.155), calls=%async_computation.1 | async-start | bytes 131072 | tf_op jit(solution)/shard_map/all_to_all | solution.py:75
  28.3 4.4 broadcast_in_dim.18
  32.7 7.9 %scatter_fusion = f32[32,256,256]{2,1,0:T(8,128)} fusion(f32[32,256,256]{2,1,0:T(8,128)} %broadcast_in_dim.18, s32[16]{0:T(128)S(1)} %fusion.31, f32[16,256,256]{2,1,0:T(8,128)} %bitcast.46), kind=kCustom, calls=%fused_computation.2 | custom fusion | bytes 12582976 | tf_op jit(solution)/shard_map/scatter | solution.py:60
  40.6 0.0 all-to-all-done.1
  40.6 7.3 %all-to-all-start.2 = ((f32[16,2,256,256]{3,2,1,0:T(8,128)}), f32[16,2,256,256]{3,2,1,0:T(8,128)}, u32[]{:S(2)}, u32[]{:S(2)}) async-start(f32[16,2,256,256]{3,2,1,0:T(8,128)} %bitcast.42), calls=%async_computation.2 | async-start | bytes 16777216 | tf_op jit(solution)/shard_map/all_to_all | solution.py:68
  47.9 0.0 all-reduce.7.cloned.1.call-start
  47.9 0.1 convert_element_type.39
  48.1 114.1 %all-to-all-done.2 = f32[16,2,256,256]{3,2,1,0:T(8,128)} async-done(((f32[16,2,256,256]{3,2,1,0:T(8,128)}), f32[16,2,256,256]{3,2,1,0:T(8,128)}, u32[]{:S(2)}, u32[]{:S(2)}) %all-to-all-start.2) | async-done | bytes 8388640 | tf_op jit(solution)/shard_map/all_to_all | solution.py:68
  162.3 8.2 %fusion.3 = f32[32,256,256]{2,1,0:T(8,128)S(1)} fusion(f32[32,256,256]{2,1,0:T(8,128)} %bitcast.11, s32[32,256]{1,0:T(8,128)S(1)} %get-tuple-element.30, pred[32]{0:T(512)(128)(4,1)S(1)} %broadcast_compare_fusion), kind=kOutput, calls=%fused_computation.10 | convolution fusion | flops 6446645248 | bytes 16810016 | tf_op jit(solution)/shard_map/sai,sij->saj/dot_general | solution.py:97
  170.5 7.3 %fusion.5 = f32[32,256,256]{2,1,0:T(8,128)} fusion(f32[32,256,256]{2,1,0:T(8,128)S(1)} %fusion.3, s32[32,256]{1,0:T(8,128)S(1)} %get-tuple-element.29), kind=kOutput, calls=%fused_computation.11 | convolution fusion | flops 6444548096 | bytes 16809984 | tf_op jit(solution)/shard_map/saj,sbj->sab/dot_general | solution.py:98
  177.8 15.6 %fusion = f32[32,256,256]{2,0,1:T(8,128)} fusion(f32[32,256,256]{2,1,0:T(8,128)} %fusion.5, s32[32]{0:T(128)S(1)} %convert_element_type.39), kind=kOutput, calls=%fused_computation.5 | convolution fusion | flops 805307392 | bytes 16777344 | tf_op jit(solution)/shard_map/sk,sab->kab/dot_general | solution.py:101
  193.3 9.7 %reshape.159 = f32[8,4,256,256]{3,1,0,2:T(4,128)} reshape(f32[32,256,256]{2,0,1:T(8,128)} %fusion) | data formatting | bytes 16777216 | tf_op jit(solution)/shard_map/reshape | solution.py:102
  203.1 8.1 %copy.15 = f32[8,256,4,256]{3,2,1,0:T(4,128)} copy(f32[8,256,4,256]{3,2,0,1:T(4,128)} %bitcast.44) | data formatting | bytes 16777216 | tf_op jit(solution)/shard_map/transpose | solution.py:102
  211.2 8.9 %copy.16 = f32[256,8,4,256]{3,1,2,0:T(8,128)} copy(f32[256,8,4,256]{3,2,1,0:T(4,128)} %bitcast.45) | data formatting | bytes 16777216
  220.1 0.0 copy-start.1
  220.1 12.2 %add.79 = f32[2048,1024]{1,0:T(8,128)} add(f32[2048,1024]{1,0:T(8,128)} %param.11, f32[2048,1024]{1,0:T(8,128)} %bitcast.43) | non-fusion elementwise | flops 2097152 | bytes 25165824 | tf_op jit(solution)/shard_map/add | solution.py:103
  232.3 2.4 slice_select_fusion.1
  234.7 0.0 all-reduce.7.cloned.1.call-update
  234.7 0.0 all-reduce.5.cloned.1.call-start
  234.7 0.0 copy-done.1
  234.7 4.7 broadcast_select_fusion.1
  239.4 0.0 all-reduce.5.cloned.1.call-update
  239.5 0.0 all-reduce.11.cloned.1.call-start
  239.5 0.9 compare_reduce_fusion.1
  240.4 63.1 %all-reduce.7.cloned.1.call-done = f32[256,1024]{1,0:T(8,128)} async-done(((f32[256,1024]{1,0:T(8,128)}), f32[256,1024]{1,0:T(8,128)}) %all-reduce.7.cloned.1.call-update) | async-done | bytes 1048592 | tf_op jit(solution)/shard_map/psum | solution.py:15
  303.6 90.8 %all-reduce.5.cloned.1.call-done = f32[2048,256]{1,0:T(8,128)} async-done(((f32[2048,256]{1,0:T(8,128)}), f32[2048,256]{1,0:T(8,128)}) %all-reduce.5.cloned.1.call-update) | async-done | bytes 2097168 | tf_op jit(solution)/shard_map/psum | solution.py:15
  394.3 10.9 %subtract_select_fusion.1 = f32[2048,1024]{1,0:T(8,128)S(1)} fusion(f32[2048,1024]{1,0:T(8,128)} %add.79, f32[2048,256]{1,0:T(8,128)} %all-reduce.5.cloned.1.call-done, f32[256,1024]{1,0:T(8,128)} %all-reduce.7.cloned.1.call-done, pred[1024]{0:T(1024)(128)(4,1)S(1)} %fusion.29, pred[2048]{0:T(1024)(128)(4,1)S(1)} %fusion.26), kind=kOutput, calls=%fused_computation.4 | convolution fusion | flops 6448742400 | bytes 19926016 | tf_op jit(solution)/shard_map/dot_general | solution.py:36
  405.3 1.2 fusion.9
  406.5 0.0 copy-start
  406.5 3.4 copy-done
  409.9 1.1 slice_select_fusion
  411.0 0.0 all-reduce.11.cloned.1.call-update
  411.0 0.0 all-reduce.9.cloned.1.call-start
  411.1 4.7 broadcast_select_fusion
  415.8 0.0 all-reduce.9.cloned.1.call-update
  415.8 0.6 compare_reduce_fusion
  416.5 58.6 %all-reduce.11.cloned.1.call-done = f32[256,1024]{1,0:T(8,128)} async-done(((f32[256,1024]{1,0:T(8,128)}), f32[256,1024]{1,0:T(8,128)}) %all-reduce.11.cloned.1.call-update) | async-done | bytes 1048592 | tf_op jit(solution)/shard_map/psum | solution.py:15
  475.0 91.0 %all-reduce.9.cloned.1.call-done = f32[2048,256]{1,0:T(8,128)} async-done(((f32[2048,256]{1,0:T(8,128)}), f32[2048,256]{1,0:T(8,128)}) %all-reduce.9.cloned.1.call-update) | async-done | bytes 2097168 | tf_op jit(solution)/shard_map/psum | solution.py:15
  566.0 12.5 %subtract_select_fusion = f32[2048,1024]{1,0:T(8,128)} fusion(f32[2048,1024]{1,0:T(8,128)} %copy-done, f32[2048,256]{1,0:T(8,128)} %all-reduce.9.cloned.1.call-done, f32[256,1024]{1,0:T(8,128)} %all-reduce.11.cloned.1.call-done, pred[1024]{0:T(1024)(128)(4,1)S(1)} %fusion.30, pred[2048]{0:T(1024)(128)(4,1)S(1)} %fusion.27), kind=kOutput, calls=%fused_computation.3 | convolution fusion | flops 6448742400 | bytes 19926016 | tf_op jit(solution)/shard_map/dot_general | solution.py:36
  578.5 3.3 fusion.10
  (11 shorter events, 0.2 us)
Async XLA Ops:
  10.1 11.7 %all-to-all-start = ((f32[16,1,2]{2,1,0:T(1,128)}), f32[16,1,2]{2,1,0:T(1,128)S(1)}, u32[]{:S(2)}, u32[]{:S(2)}) async-start(f32[16,1,2]{2,1,0:T(1,128)} %bitcast.5), calls=%async_computation | async-start | bytes 16384 | tf_op jit(solution)/shard_map/all_to_all | solution.py:82
  21.8 18.8 %all-to-all-start.1 = ((f32[16,2,512]{2,1,0:T(2,128)}), f32[16,2,512]{2,1,0:T(2,128)S(1)}, u32[]{:S(2)}, u32[]{:S(2)}) async-start(f32[16,2,512]{2,1,0:T(2,128)} %reshape.155), calls=%async_computation.1 | async-start | bytes 131072 | tf_op jit(solution)/shard_map/all_to_all | solution.py:75
  40.6 121.7 %all-to-all-start.2 = ((f32[16,2,256,256]{3,2,1,0:T(8,128)}), f32[16,2,256,256]{3,2,1,0:T(8,128)}, u32[]{:S(2)}, u32[]{:S(2)}) async-start(f32[16,2,256,256]{3,2,1,0:T(8,128)} %bitcast.42), calls=%async_computation.2 | async-start | bytes 16777216 | tf_op jit(solution)/shard_map/all_to_all | solution.py:68
  47.9 255.7 %all-reduce.7.cloned.1.call-start = ((), (), s32[]{:S(2)}) async-start(), calls=%async_computation.4 | async-start | bytes 2097152 | tf_op jit(solution)/shard_map/psum | solution.py:15
  220.1 14.6 %copy-start.1 = (f32[2,256,256]{2,1,0:T(8,128)S(1)}, f32[2,256,256]{2,1,0:T(8,128)}, u32[]{:S(2)}) copy-start(f32[2,256,256]{2,1,0:T(8,128)} %param.17) | copy-start | bytes 1572868
  234.7 159.7 %all-reduce.5.cloned.1.call-start = ((), (), s32[]{:S(2)}) async-start(), calls=%async_computation.3 | async-start | bytes 4194304 | tf_op jit(solution)/shard_map/psum | solution.py:15
  239.5 235.6 %all-reduce.11.cloned.1.call-start = ((), (), s32[]{:S(2)}) async-start(), calls=%async_computation.6 | async-start | bytes 2097152 | tf_op jit(solution)/shard_map/psum | solution.py:15
  406.5 3.4 copy-start
  411.0 155.0 %all-reduce.9.cloned.1.call-start = ((), (), s32[]{:S(2)}) async-start(), calls=%async_computation.5 | async-start | bytes 4194304 | tf_op jit(solution)/shard_map/psum | solution.py:15
Sparse Core Ops, SparseCore 0:
  234.8 68.7 all-reduce.6
  306.9 87.4 all-reduce.4
  411.1 63.8 all-reduce.10
  478.5 87.4 all-reduce.8
where the time goes:
time: 591 us; the launch traced here: 588 us
  waiting for transfers between devices  420 us (71%)
  matrix products  63.8 us (11%)
  local copies, waits for them, and re-layouts  44.5 us (8%)
  other arithmetic  24.9 us (4%)
  starting transfers between devices  21.3 us (4%)
  between operations  13.3 us (2%)
    psum x4, waiting for transfers between devices, broadcast(): return lax.psum(jnp.where(mine, array, jnp.zeros_like(array)), axis)  303 us
    all_to_all x1, waiting for transfers between devices, per_device(): lax.all_to_all(sent_tiles.reshape(col_total, CAP, tile_size, tile_size),...  114 us
    dot_general x2, matrix products, eliminate(): update = jnp.dot(left_factor, right_factor, precision=highest_precision)  23.4 us
    dot_general x1, matrix products, per_device(): jnp.einsum('sk,sab->kab', tile_onehot, arranged, precision=highest_precis...  15.6 us
    unnamed x5, local copies, waits for them, and re-layouts  12.3 us
    add x1, other arithmetic, per_device(): front_matrix = front_matrix + summed.reshape(front_matrix.shape)  12.2 us
  transfers between devices with their start and end apart: 7, of which 6 were waited for; matrix products, arithmetic and copies ran while one was open for 4% of the time, Pallas kernels for 0%

commit v1 on v0

v1 whole, which is shorter than its diff:
```python
import functools
import jax
import jax.numpy as jnp
from jax import lax
from jax.experimental import pallas as pl
from jax.experimental.pallas import tpu as pltpu
from jax.sharding import PartitionSpec as P

TILE = 256
SLOT = TILE + 8
CAP = 2
N_ROW = 8
N_COL = 16
MESH = pl.DeviceIdType.MESH
DMA = pltpu.SemaphoreType.DMA
ANY = pl.BlockSpec(memory_space=pl.ANY)


def halves(value):
    high = value.astype(jnp.bfloat16)
    low = (value - high.astype(jnp.float32)).astype(jnp.bfloat16)
    return high, low


def product(left, right, dims=(((1,), (0,)), ((), ()))):
    return lax.dot_general(left, right, dims, preferred_element_type=jnp.float32)


def product3(left, right):
    left_high, left_low = left
    right_high, right_low = right
    return (
        product(left_high, right_high)
        + product(left_high, right_low)
        + product(left_low, right_high)
    )


def permute_kernel(source, mark, tile, row_map, col_map, out):
    slot = pl.program_id(0)

    @pl.when(mark[slot] >= 0)
    def _():
        order = lax.broadcasted_iota(jnp.int32, (TILE, TILE), 0)
        to_row = (order == row_map[0]).astype(jnp.bfloat16)
        to_col = (order == col_map[0]).astype(jnp.bfloat16)
        across = (((1,), (1,)), ((), ()))
        result = None
        for part in halves(tile[0]):
            moved = product(part, to_col, across).astype(jnp.bfloat16)
            moved = product(to_row, moved)
            result = moved if result is None else result + moved
        out[0, :TILE, :] = result

    out[0, TILE:, :] = jnp.full((8, TILE), mark[slot].astype(jnp.float32))


def permute(source, mark, tiles, row_map, col_map):
    slots = source.shape[0]
    count = tiles.shape[0]
    return pl.pallas_call(
        permute_kernel,
        out_shape=jax.ShapeDtypeStruct((slots, SLOT, TILE), jnp.float32),
        grid_spec=pltpu.PrefetchScalarGridSpec(
            num_scalar_prefetch=2,
            grid=(slots,),
            in_specs=[
                pl.BlockSpec((1, TILE, TILE), lambda s, src, mk: (src[s], 0, 0)),
                pl.BlockSpec((1, 1, TILE), lambda s, src, mk: (src[s], 0, 0)),
                pl.BlockSpec((1, 1, TILE), lambda s, src, mk: (src[s], 0, 0)),
            ],
            out_specs=pl.BlockSpec((1, SLOT, TILE), lambda s, src, mk: (s, 0, 0)),
        ),
        name="permute",
    )(source, mark, tiles, row_map.reshape(count, 1, TILE), col_map.reshape(count, 1, TILE))


NEAR = [(1, 0), (3, 0), (0, 1), (0, 3), (1, 1), (3, 3), (1, 3), (3, 1)]
FAR = [(2, 0), (0, 2), (2, 2), (2, 1), (2, 3), (1, 2), (3, 2)]


def cut(rows, parts):
    edges = [rows // 8 * i // parts * 8 for i in range(parts + 1)]
    return [(edges[i], edges[i + 1] - edges[i]) for i in range(parts)]


def exchange_kernel(sent, got, relay, own_sem, s1, r1, s2, r2, s3, r3):
    row = lax.axis_index("row")
    col = lax.axis_index("col")
    y, x = col // 4, col % 4
    rows = sent.shape[1]

    def at(dx, dy):
        return (y + dy) % 4 * 4 + (x + dx) % 4

    barrier = pltpu.get_barrier_semaphore()
    for offset in NEAR:
        pl.semaphore_signal(barrier, inc=1, device_id=(row, at(*offset)), device_id_type=MESH)
    pl.semaphore_wait(barrier, len(NEAR))
    own = pltpu.make_async_copy(sent.at[col], got.at[col], own_sem)
    own.start()
    legs = []
    for i, (dx, dy) in enumerate(FAR):
        for half, (first, count) in enumerate(cut(rows, 2)):
            step = 1 if half == 0 else 3
            rx, ry = (step if dx == 2 else 0), (step if dy == 2 else 0)
            j = 2 * i + half
            leg = pltpu.make_async_remote_copy(
                src_ref=sent.at[at(dx, dy), pl.ds(first, count)],
                dst_ref=relay.at[j, pl.ds(0, count)],
                send_sem=s2.at[j],
                recv_sem=r2.at[j],
                device_id=(row, at(rx, ry)),
                device_id_type=MESH,
            )
            leg.start()
            legs.append((leg, j, at(-rx, -ry), at(dx - rx, dy - ry), first, count))
    straight = []
    for i, (dx, dy) in enumerate(NEAR):
        copy = pltpu.make_async_remote_copy(
            src_ref=sent.at[at(dx, dy)],
            dst_ref=got.at[col],
            send_sem=s1.at[i],
            recv_sem=r1.at[i],
            device_id=(row, at(dx, dy)),
            device_id_type=MESH,
        )
        straight.append(copy)
    for copy in straight[:4]:
        copy.start()
    onward = []
    for leg, j, origin, target, first, count in legs:
        leg.wait_recv()
        copy = pltpu.make_async_remote_copy(
            src_ref=relay.at[j, pl.ds(0, count)],
            dst_ref=got.at[origin, pl.ds(first, count)],
            send_sem=s3.at[j],
            recv_sem=r3.at[j],
            device_id=(row, target),
            device_id_type=MESH,
        )
        copy.start()
        onward.append(copy)
    for copy in straight[4:]:
        copy.start()
    for copy in straight + onward:
        copy.wait()
    for leg, *_ in legs:
        leg.wait_send()
    own.wait()


def exchange(sent):
    rows = sent.shape[1]
    return pl.pallas_call(
        exchange_kernel,
        out_shape=jax.ShapeDtypeStruct(sent.shape, jnp.float32),
        in_specs=[ANY],
        out_specs=ANY,
        scratch_shapes=[pltpu.VMEM((2 * len(FAR), cut(rows, 2)[1][1], TILE), jnp.float32), DMA]
        + [DMA((len(NEAR),))] * 2
        + [DMA((2 * len(FAR),))] * 4,
        compiler_params=pltpu.CompilerParams(collective_id=1, has_side_effects=True),
        name="exchange",
    )(sent)


def assemble_kernel(target, front, got, out):
    band = pl.program_id(0)
    out[...] = front[...]
    for slot in range(target.shape[0]):
        place = target[slot]

        @pl.when((place >= 0) & (place // 4 == band))
        def _():
            lanes = pl.ds(pl.multiple_of(place % 4 * TILE, TILE), TILE)
            out[:, lanes] += got[slot // CAP, pl.ds(slot % CAP * SLOT, TILE), :]


def assemble(target, front, got):
    rows, cols = front.shape
    return pl.pallas_call(
        assemble_kernel,
        out_shape=jax.ShapeDtypeStruct(front.shape, jnp.float32),
        grid_spec=pltpu.PrefetchScalarGridSpec(
            num_scalar_prefetch=1,
            grid=(rows // TILE,),
            in_specs=[
                pl.BlockSpec((TILE, cols), lambda i, t: (i, 0)),
                pl.BlockSpec(got.shape, lambda i, t: (0, 0, 0), pipeline_mode=pl.Buffered(1)),
            ],
            out_specs=pl.BlockSpec((TILE, cols), lambda i, t: (i, 0)),
        ),
        name="assemble",
    )(target, front, got)


PIECE = 32
PIECES = 16
BAND = 16
CORNER_AT = 10


def spanning_trees():
    trees = []
    for tree in range(4):
        depth, edges = {}, []

        def grow(node, last, level):
            depth[node] = level
            for turn in range(last + 1, 4):
                bit = ((turn + 1) % 4 + tree) % 4
                child = node ^ (1 << bit)
                if child != 0:
                    edges.append((node, bit))
                    grow(child, turn, level + 1)

        grow(1 << tree, -1, 1)
        edges.append((0, tree))
        trees.append((depth, edges))
    return trees


def gray(column):
    y, x = column // 4, column % 4
    return (x ^ (x >> 1)) + 4 * (y ^ (y >> 1))


def panel_kernel(front, block, band, corner, ts, tr, cs, cr, us, ur, qs, qr, vs, vr, ws, wr):
    row = lax.axis_index("row")
    col = lax.axis_index("col")
    y, x = col // 4, col % 4
    z, core = row // 2, row % 2
    beside = [
        (row, y * 4 + (x + 1 - 2 * (x % 2))),
        (row, y * 4 + 3 - x),
        (row, (y + 1 - 2 * (y % 2)) * 4 + x),
        (row, (3 - y) * 4 + x),
    ]
    along = [((z + 1) % 4 * 2 + core, col), ((z + 3) % 4 * 2 + core, col)]
    partner = (z * 2 + 1 - core, col)
    barrier = pltpu.get_barrier_semaphore()
    for device in beside + along + [partner]:
        pl.semaphore_signal(barrier, inc=1, device_id=device, device_id_type=MESH)
    pl.semaphore_wait(barrier, 7)

    trees = spanning_trees()
    names = {gray(column): column for column in range(N_COL)}
    level, sends = [], []
    for depth, edges in trees:
        at = jnp.int32(0)
        for node, steps in depth.items():
            at = at + jnp.where(col == names[node], steps, 0)
        level.append(at)
        by_bit = {}
        for bit in range(4):
            nodes = [names[node] for node, b in edges if b == bit and node != 0]
            if nodes:
                by_bit[bit] = functools.reduce(jnp.logical_or, [col == node for node in nodes])
        sends.append(by_bit)
    root = col == 0
    upper = row == 0
    leads = core == 0
    way = [z, (4 - z) % 4]

    def remote(source, target, send, receive, device):
        return pltpu.make_async_remote_copy(
            src_ref=source,
            dst_ref=target,
            send_sem=send,
            recv_sem=receive,
            device_id=device,
            device_id_type=MESH,
        )

    def block_piece(tree, piece):
        return block.at[pl.ds(pl.multiple_of((piece * 4 + tree) * PIECE, PIECE), PIECE)]

    def block_copy(tree, bit, piece, source):
        return remote(
            source, block_piece(tree, piece), ts.at[tree, bit], tr.at[tree, piece], beside[bit]
        )

    def corner_copy(tree, bit, source):
        target = corner.at[pl.ds(tree * 64, 64)]
        return remote(source, target, cs.at[tree, bit], cr.at[tree], beside[bit])

    def front_piece(tree, piece):
        first = pl.multiple_of((piece * 4 + tree) * PIECE, PIECE)
        return front.at[pl.ds(first, PIECE), pl.ds(0, 2 * TILE)]

    def band_piece(ref, half, piece):
        return ref.at[pl.ds(pl.multiple_of(half * TILE + piece * BAND, BAND), BAND)]

    def corner_half(half):
        return corner.at[pl.ds(half * TILE, TILE)]

    def step(now, carry):
        for tree in range(4):
            piece = now - level[tree] - 1

            @pl.when((piece == -1) & upper)
            def _():
                @pl.when(root)
                def _():
                    source = front.at[pl.ds(tree * 64, 64), pl.ds(TILE, TILE)]
                    corner_copy(tree, tree, source).start()

                @pl.when(jnp.logical_not(root))
                def _():
                    source = corner.at[pl.ds(tree * 64, 64)]
                    corner_copy(tree, 0, source).wait_recv()
                    for bit, here in sends[tree].items():

                        @pl.when(here)
                        def _():
                            corner_copy(tree, bit, source).start()

            @pl.when((piece >= 0) & (piece < PIECES))
            def _():
                @pl.when(root)
                def _():
                    block_copy(tree, tree, piece, front_piece(tree, piece)).start()

                @pl.when(jnp.logical_not(root))
                def _():
                    source = block_piece(tree, piece)
                    block_copy(tree, 0, piece, source).wait_recv()
                    for bit, here in sends[tree].items():

                        @pl.when(here)
                        def _():
                            block_copy(tree, bit, piece, source).start()

        for half in range(2):
            hops = way[half]
            piece = now - hops

            def band_copy(source, which):
                target = band_piece(band, half, piece)
                if which == 0:
                    return remote(source, target, us.at[half], ur.at[half, piece], along[half])
                return remote(source, target, qs.at[half], qr.at[half], partner)

            @pl.when(leads & (piece >= 0) & (piece < PIECES))
            def _():
                @pl.when(hops == 0)
                def _():
                    source = band_piece(front, half, piece)
                    band_copy(source, 0).start()
                    band_copy(source, 1).start()

                @pl.when(hops > 0)
                def _():
                    source = band_piece(band, half, piece)
                    band_copy(source, 0).wait_recv()

                    @pl.when(hops < 3)
                    def _():
                        band_copy(source, 0).start()

                    band_copy(source, 1).start()

            def pass_on(source):
                @pl.when(hops < 3)
                def _():
                    remote(source, corner_half(half), vs.at[half], vr.at[half], along[half]).start()

                remote(source, corner_half(half), ws.at[half], wr.at[half], partner).start()

            @pl.when(leads & (now == CORNER_AT + 3 * hops))
            def _():
                @pl.when(upper & root)
                def _():
                    if half == 0:
                        pass_on(front.at[pl.ds(0, TILE), pl.ds(TILE, TILE)])
                    else:
                        pass_on(front.at[pl.ds(TILE, TILE), pl.ds(0, TILE)])

                @pl.when(upper & jnp.logical_not(root))
                def _():
                    if half == 0:
                        pass_on(corner_half(0))
                    else:
                        pass_on(block.at[pl.ds(TILE, TILE), pl.ds(0, TILE)])

                @pl.when(jnp.logical_not(upper))
                def _():
                    source = corner_half(half)
                    remote(source, source, vs.at[half], vr.at[half], along[half]).wait_recv()
                    pass_on(source)

        return carry

    lax.fori_loop(0, PIECES + 6, step, 0)

    whole = block.at[pl.ds(0, PIECE * PIECES)]
    for tree in range(4):

        def sent(bit):
            remote(whole, whole, ts.at[tree, bit], tr.at[tree, 0], beside[bit]).wait_send()

            @pl.when(upper)
            def _():
                corner_copy(tree, bit, corner.at[pl.ds(tree * 64, 64)]).wait_send()

        @pl.when(root)
        def _():
            sent(tree)

        for bit, here in sends[tree].items():

            @pl.when(here)
            def _():
                sent(bit)

    for half in range(2):
        whole_band = band.at[pl.ds(half * TILE, TILE)]
        band_along = remote(whole_band, whole_band, us.at[half], ur.at[half, 0], along[half])
        band_beside = remote(whole_band, whole_band, qs.at[half], qr.at[half], partner)
        ends = corner_half(half)
        corner_along = remote(ends, ends, vs.at[half], vr.at[half], along[half])
        corner_beside = remote(ends, ends, ws.at[half], wr.at[half], partner)

        @pl.when(leads)
        def _():
            @pl.when(way[half] < 3)
            def _():
                band_along.wait_send()
                corner_along.wait_send()

            band_beside.wait_send()
            corner_beside.wait_send()

        @pl.when(jnp.logical_not(leads))
        def _():
            band_beside.wait_recv()
            corner_beside.wait_recv()


def share_panels(front):
    rows, cols = front.shape
    return pl.pallas_call(
        panel_kernel,
        out_shape=(
            jax.ShapeDtypeStruct((rows, 2 * TILE), jnp.float32),
            jax.ShapeDtypeStruct((2 * TILE, cols), jnp.float32),
            jax.ShapeDtypeStruct((2 * TILE, TILE), jnp.float32),
        ),
        in_specs=[ANY],
        out_specs=(ANY,) * 3,
        scratch_shapes=[
            DMA((4, 4)),
            DMA((4, PIECES)),
            DMA((4, 4)),
            DMA((4,)),
            DMA((2,)),
            DMA((2, PIECES)),
        ]
        + [DMA((2,))] * 6,
        compiler_params=pltpu.CompilerParams(collective_id=2, has_side_effects=True),
        name="share_panels",
    )(front)


def update_kernel(
    front, block, band, corner, top, side, inverse, out, up_high, up_low, small_high, small_low
):
    step = pl.program_id(0)
    row = lax.axis_index("row")
    root = lax.axis_index("col") == 0
    upper = row == 0

    @pl.when(step == 0)
    def _():
        band_now = jnp.where(upper, top[...], band[...])
        right = jnp.where(upper & root, top[:TILE, TILE : 2 * TILE], corner[:TILE])
        below = jnp.where(root, top[TILE:, :TILE], side[...])
        below = jnp.where(upper, below, corner[TILE:])
        for place, value in enumerate((inverse[0], inverse[1], right)):
            small_high[place], small_low[place] = halves(value)
        first = band_now[:TILE]
        first_parts = halves(first)
        ratio = product3(halves(below), (small_high[0], small_low[0]))
        second = band_now[TILE:] - product3(halves(ratio), first_parts)
        up_high[:TILE], up_low[:TILE] = first_parts
        up_high[TILE:], up_low[TILE:] = halves(second)

    current = front[...]
    columns = jnp.where(root, current[:, : 2 * TILE], block[...])
    lower_0 = product3(halves(columns[:, :TILE]), (small_high[0], small_low[0]))
    lower_0_parts = halves(lower_0)
    rest = columns[:, TILE:] - product3(lower_0_parts, (small_high[2], small_low[2]))
    lower_1 = product3(halves(rest), (small_high[1], small_low[1]))
    number = row * (N_ROW * TILE // TILE) + step
    live_0 = number >= 1
    live_1 = number >= 2
    both = jnp.concatenate(
        [jnp.where(live_0, lower_0, 0.0), jnp.where(live_1, lower_1, 0.0)], axis=1
    )
    high, low = halves(both)
    update = product3((high, low), (up_high[...], up_low[...]))
    out[...] = current - update

    @pl.when(root & live_0)
    def _():
        out[:, :TILE] = lower_0

    @pl.when(root & live_1)
    def _():
        out[:, TILE : 2 * TILE] = lower_1


def update(front, block, band, corner, inverse):
    rows, cols = front.shape
    once = pl.Buffered(1)
    return pl.pallas_call(
        update_kernel,
        out_shape=jax.ShapeDtypeStruct(front.shape, jnp.float32),
        grid=(rows // TILE,),
        in_specs=[
            pl.BlockSpec((TILE, cols), lambda i: (i, 0)),
            pl.BlockSpec((TILE, 2 * TILE), lambda i: (i, 0)),
            pl.BlockSpec((2 * TILE, cols), lambda i: (0, 0), pipeline_mode=once),
            pl.BlockSpec((2 * TILE, TILE), lambda i: (0, 0), pipeline_mode=once),
            pl.BlockSpec((2 * TILE, cols), lambda i: (0, 0), pipeline_mode=once),
            pl.BlockSpec((TILE, TILE), lambda i: (1, 0), pipeline_mode=once),
            pl.BlockSpec((2, TILE, TILE), lambda i: (0, 0, 0), pipeline_mode=once),
        ],
        out_specs=pl.BlockSpec((TILE, cols), lambda i: (i, 0)),
        scratch_shapes=[pltpu.VMEM((2 * TILE, cols), jnp.bfloat16)] * 2
        + [pltpu.VMEM((3, TILE, TILE), jnp.bfloat16)] * 2,
        name="update",
    )(front, block, band, corner, front, block, inverse)


def per_device(
    front_matrix, child_tiles, target_column, target_tile, row_map, col_map, pivot_inverse
):
    count = child_tiles.shape[2]
    targets = target_column.reshape(count)
    numbers = jnp.arange(count, dtype=jnp.int32)
    earlier = (targets[:, None] == targets[None, :]) & (numbers[None, :] < numbers[:, None])
    placed = targets * CAP + jnp.sum(earlier.astype(jnp.int32), axis=1)
    slots = jnp.arange(N_COL * CAP, dtype=jnp.int32)
    match = placed[None, :] == slots[:, None]
    source = jnp.sum(jnp.where(match, numbers[None, :], 0), axis=1)
    mark = jnp.sum(jnp.where(match, target_tile.reshape(1, count) + 1, 0), axis=1) - 1
    sent = permute(
        source,
        mark,
        child_tiles.reshape(count, TILE, TILE),
        row_map.reshape(count, TILE),
        col_map.reshape(count, TILE),
    )
    got = exchange(sent.reshape(N_COL, CAP * SLOT, TILE))
    target = got.reshape(N_COL * CAP, SLOT, TILE)[:, TILE, 0].astype(jnp.int32)
    front = assemble(target, front_matrix, got)
    block, band, corner = share_panels(front)
    return update(front, block, band, corner, pivot_inverse)


def solution(mesh):
    in_specs = (
        P("row", "col"),
        P("row", "col", None, None, None),
        P("row", "col", None, None),
        P("row", "col", None),
        P("row", "col", None, None),
        P("row", "col", None, None),
        P(),
    )
    return jax.shard_map(
        per_device, mesh=mesh, in_specs=in_specs, out_specs=P("row", "col"), check_vma=False
    )
```

time: 591 us -> 276 us (0.47)
  waiting for transfers between devices: 420 us -> 0 us
  Pallas kernels: 0 us -> 268 us
  matrix products: 63.8 us -> 0 us
  local copies, waits for them, and re-layouts: 44.5 us -> 3.65 us
  starting transfers between devices: 21.3 us -> 0 us
  other arithmetic: 24.9 us -> 3.86 us
  between operations: 13.3 us -> 0.03 us
    psum x4 -> x0, waiting for transfers between devices: 303 us -> none  [broadcast(): return lax.psum(jnp.where(mine, array, jnp.zeros_like(array)), axis)]
    pallas_call x0 -> x5, Pallas kernels: none -> 268 us  [the longest x1 122 us: exchange(): pl.pallas_call(exchange_kernel, out_shape=jax.ShapeDtypeStruct(sent.shape...]
    all_to_all x3 -> x0, waiting for transfers between devices: 117 us -> none  [the longest x1 114 us: per_device(): lax.all_to_all(sent_tiles.reshape(col_total, CAP, tile_size, tile_size),...]
    dot_general x7 -> x0, matrix products: 63.8 us -> none  [the longest x2 23.4 us: eliminate(): update = jnp.dot(left_factor, right_factor, precision=highest_precision)]
    all_to_all x3 -> x0, starting transfers between devices: 21.1 us -> none  [the longest x1 7.34 us: per_device(): lax.all_to_all(sent_index.reshape(col_total, CAP), 'col', split_axis=0, c...]
    unnamed x5 -> x1, local copies, waits for them, and re-layouts: 12.3 us -> 0.08 us
    add x1 -> x2, other arithmetic: 12.2 us -> 1.32 us  [the longest x1 0.66 us: per_device(): placed = targets * CAP + jnp.sum(earlier.astype(jnp.int32), axis=1)]
    reshape x2 -> x0, local copies, waits for them, and re-layouts: 10.4 us -> none  [the longest x1 9.75 us: per_device(): summed.reshape(tile_rows, tile_cols, tile_size, tile_size)]
  transfers between devices with their start and end apart: 7 -> 0, of which waited for: 6 -> 0; matrix products, arithmetic and copies ran while one was open for 4% -> 0% of each run, Pallas kernels for 0% -> 0%
where the time goes in v1:
time: 276 us; the launch traced here: 275 us
  Pallas kernels  268 us (97%)
  other arithmetic  3.86 us (1%)
  local copies, waits for them, and re-layouts  3.65 us (1%)
    pallas_call x1, Pallas kernels, exchange(): pl.pallas_call(exchange_kernel, out_shape=jax.ShapeDtypeStruct(sent.shape...  122 us
    pallas_call x1, Pallas kernels, share_panels(): pl.pallas_call(panel_kernel, out_shape=(jax.ShapeDtypeStruct((rows, 2 * T...  82.2 us
    pallas_call x1, Pallas kernels, permute(): pl.pallas_call(permute_kernel, out_shape=jax.ShapeDtypeStruct((slots, SLO...  27.3 us
    pallas_call x1, Pallas kernels, update(): pl.pallas_call(update_kernel, out_shape=jax.ShapeDtypeStruct(front.shape,...  22.5 us
    pallas_call x1, Pallas kernels, assemble(): pl.pallas_call(assemble_kernel, out_shape=jax.ShapeDtypeStruct(front.shap...  13.9 us

profile of v1, /device:TPU:12, one launch (start us, length us, event | category | flops | bytes accessed | tf_op | source)
XLA Modules:
  0.0 275.5 jit_solution(1452975752260405595)
XLA Ops:
  0.0 0.7 add_bitcast_fusion
  0.7 0.9 convert_reduce_fusion
  1.6 0.7 multiply_add_fusion
  2.2 0.6 select_reduce_fusion
  2.8 0.5 broadcast_add_fusion.mark
  3.3 1.3 reshape_reshape.6.row_map
  4.7 1.3 reshape_reshape.7.col_map
  6.0 27.3 %permute.1 = f32[32,264,256]{2,1,0:T(8,128)} custom-call(s32[32]{0:T(128)} %get-tuple-element.12.source, s32[32]{0:T(128)} %broadcast_add_fusion.mark, f32[16,256,256]{2,1,0:T(8,128)} %bitcast.15, s32[16,1,256]{2,1,0:T(1,128)} %reshape_reshape.6.row_map, s32[16,1,256]{2,1,0:T(1,128)} %reshape_reshape.7.col_map), custom_call_target="tpu_custom_call" | custom-call | tf_op jit(solution)/shard_map/permute/pallas_call | solution.py:61
  33.3 122.0 %exchange.1.got = f32[16,528,256]{2,1,0:T(8,128)} custom-call(f32[16,528,256]{2,1,0:T(8,128)} %bitcast.14), custom_call_target="tpu_custom_call" | custom-call | tf_op jit(solution)/shard_map/exchange/pallas_call | solution.py:155
  155.3 0.9 slice.4
  156.2 0.1 copy.10
  156.3 0.5 convert_bitcast_fusion.target
  156.8 13.9 %assemble.1.front.top = f32[2048,1024]{1,0:T(8,128)} custom-call(s32[32]{0:T(128)} %convert_bitcast_fusion.target, f32[2048,1024]{1,0:T(8,128)} %front.1, f32[16,528,256]{2,1,0:T(8,128)} %exchange.1.got), custom_call_target="tpu_custom_call" | custom-call | tf_op jit(solution)/shard_map/assemble/pallas_call | solution.py:182
  170.7 82.2 %share_panels.1 = (f32[2048,512]{1,0:T(8,128)}, f32[512,1024]{1,0:T(8,128)}, f32[512,256]{1,0:T(8,128)}) custom-call(f32[2048,1024]{1,0:T(8,128)} %assemble.1.front.top), custom_call_target="tpu_custom_call" | custom-call | tf_op jit(solution)/shard_map/share_panels/pallas_call | solution.py:443
  253.0 22.5 %update.1 = f32[2048,1024]{1,0:T(8,128)} custom-call(f32[2048,1024]{1,0:T(8,128)} %assemble.1.front.top, f32[2048,512]{1,0:T(8,128)} %get-tuple-element.8.block.side, f32[512,1024]{1,0:T(8,128)} %get-tuple-element.9.band, f32[512,256]{1,0:T(8,128)} %get-tuple-element.10.corner, f32[2048,1024]{1,0:T(8,128)} %assemble.1.front.top, ...), custom_call_target="tpu_custom_call" | custom-call | tf_op jit(solution)/shard_map/update/pallas_call | solution.py:517

commit v2 on v1

--- a/solution.py
+++ b/solution.py
@@ -8,7 +8,6 @@
 
 TILE = 256
 SLOT = TILE + 8
-CAP = 2
 N_ROW = 8
 N_COL = 16
 MESH = pl.DeviceIdType.MESH
@@ -36,43 +35,74 @@
     )
 
 
-def permute_kernel(source, mark, tile, row_map, col_map, out):
-    slot = pl.program_id(0)
-
-    @pl.when(mark[slot] >= 0)
+GROUP = 8
+
+
+def plan(target_column, first, second):
+    for column in range(N_COL):
+        first[column] = -1
+        second[column] = -1
+    for tile in range(target_column.shape[0]):
+        column = target_column[tile]
+        held = first[column]
+        second[column] = jnp.where(held >= 0, tile, -1)
+        first[column] = jnp.where(held >= 0, held, tile)
+
+
+def permute_kernel(target_column, target_tile, tiles, row_map, col_map, out, first, second):
+    step = pl.program_id(0)
+
+    @pl.when(step == 0)
     def _():
-        order = lax.broadcasted_iota(jnp.int32, (TILE, TILE), 0)
-        to_row = (order == row_map[0]).astype(jnp.bfloat16)
-        to_col = (order == col_map[0]).astype(jnp.bfloat16)
-        across = (((1,), (1,)), ((), ()))
-        result = None
-        for part in halves(tile[0]):
-            moved = product(part, to_col, across).astype(jnp.bfloat16)
-            moved = product(to_row, moved)
-            result = moved if result is None else result + moved
-        out[0, :TILE, :] = result
-
-    out[0, TILE:, :] = jnp.full((8, TILE), mark[slot].astype(jnp.float32))
-
-
-def permute(source, mark, tiles, row_map, col_map):
-    slots = source.shape[0]
+        plan(target_column, first, second)
+
+    order = lax.broadcasted_iota(jnp.int32, (TILE, TILE), 0)
+    across = (((1,), (1,)), ((), ()))
+
+    def place(lane, tile):
+        there = jnp.maximum(tile, 0)
+        mark = jnp.where(tile >= 0, target_tile[there], -1)
+        to_row = (order == row_map[pl.ds(there, 1), :]).astype(jnp.bfloat16)
+        to_col = (order == col_map[pl.ds(there, 1), :]).astype(jnp.bfloat16)
+        parts = jnp.concatenate(halves(tiles[there]), axis=0)
+        moved = product(parts, to_col, across).astype(jnp.bfloat16)
+        out[lane, :TILE, :] = product(to_row, moved[:TILE]) + product(to_row, moved[TILE:])
+        out[lane, TILE:, :] = jnp.full((8, TILE), mark.astype(jnp.float32))
+
+    for pair in range(GROUP // 2):
+        place(2 * pair, first[step * (GROUP // 2) + pair])
+    for pair in range(GROUP // 2):
+        tile = second[step * (GROUP // 2) + pair]
+        out[2 * pair + 1, TILE:, :] = jnp.full((8, TILE), -1.0, jnp.float32)
+
+        @pl.when(tile >= 0)
+        def _():
+            place(2 * pair + 1, tile)
+
+
+def permute(target_column, target_tile, tiles, row_map, col_map):
+    slots = 2 * N_COL
     count = tiles.shape[0]
+    once = pl.Buffered(1)
     return pl.pallas_call(
         permute_kernel,
         out_shape=jax.ShapeDtypeStruct((slots, SLOT, TILE), jnp.float32),
         grid_spec=pltpu.PrefetchScalarGridSpec(
             num_scalar_prefetch=2,
-            grid=(slots,),
+            grid=(slots // GROUP,),
             in_specs=[
-                pl.BlockSpec((1, TILE, TILE), lambda s, src, mk: (src[s], 0, 0)),
-                pl.BlockSpec((1, 1, TILE), lambda s, src, mk: (src[s], 0, 0)),
-                pl.BlockSpec((1, 1, TILE), lambda s, src, mk: (src[s], 0, 0)),
+                pl.BlockSpec((count, TILE, TILE), lambda s, a, b: (0, 0, 0), pipeline_mode=once),
+                pl.BlockSpec((count, TILE), lambda s, a, b: (0, 0), pipeline_mode=once),
+                pl.BlockSpec((count, TILE), lambda s, a, b: (0, 0), pipeline_mode=once),
             ],
-            out_specs=pl.BlockSpec((1, SLOT, TILE), lambda s, src, mk: (s, 0, 0)),
+            out_specs=pl.BlockSpec((GROUP, SLOT, TILE), lambda s, a, b: (s, 0, 0)),
+            scratch_shapes=[
+                pltpu.SMEM((N_COL,), jnp.int32),
+                pltpu.SMEM((N_COL,), jnp.int32),
+            ],
         ),
         name="permute",
-    )(source, mark, tiles, row_map.reshape(count, 1, TILE), col_map.reshape(count, 1, TILE))
+    )(target_column, target_tile, tiles, row_map, col_map)
 
 
 NEAR = [(1, 0), (3, 0), (0, 1), (0, 3), (1, 1), (3, 3), (1, 3), (3, 1)]
@@ -88,61 +118,56 @@
     row = lax.axis_index("row")
     col = lax.axis_index("col")
     y, x = col // 4, col % 4
-    rows = sent.shape[1]
 
     def at(dx, dy):
         return (y + dy) % 4 * 4 + (x + dx) % 4
 
+    peers = [at(dx, dy) for dx, dy in NEAR + FAR]
     barrier = pltpu.get_barrier_semaphore()
-    for offset in NEAR:
-        pl.semaphore_signal(barrier, inc=1, device_id=(row, at(*offset)), device_id_type=MESH)
-    pl.semaphore_wait(barrier, len(NEAR))
+    for peer in peers:
+        pl.semaphore_signal(barrier, inc=1, device_id=(row, peer), device_id_type=MESH)
+    pl.semaphore_wait(barrier, len(peers))
+
+    def remote(source, target, send, receive, device):
+        return pltpu.make_async_remote_copy(
+            src_ref=source,
+            dst_ref=target,
+            send_sem=send,
+            recv_sem=receive,
+            device_id=(row, device),
+            device_id_type=MESH,
+        )
+
     own = pltpu.make_async_copy(sent.at[col], got.at[col], own_sem)
     own.start()
     legs = []
     for i, (dx, dy) in enumerate(FAR):
-        for half, (first, count) in enumerate(cut(rows, 2)):
+        for half, (first, size) in enumerate(cut(2 * SLOT, 2)):
             step = 1 if half == 0 else 3
             rx, ry = (step if dx == 2 else 0), (step if dy == 2 else 0)
             j = 2 * i + half
-            leg = pltpu.make_async_remote_copy(
-                src_ref=sent.at[at(dx, dy), pl.ds(first, count)],
-                dst_ref=relay.at[j, pl.ds(0, count)],
-                send_sem=s2.at[j],
-                recv_sem=r2.at[j],
-                device_id=(row, at(rx, ry)),
-                device_id_type=MESH,
+            leg = remote(
+                sent.at[at(dx, dy), pl.ds(first, size)], relay.at[j], s2.at[j], r2.at[j], at(rx, ry)
             )
             leg.start()
-            legs.append((leg, j, at(-rx, -ry), at(dx - rx, dy - ry), first, count))
+            legs.append((leg, j, at(-rx, -ry), at(dx - rx, dy - ry), first, size))
     straight = []
     for i, (dx, dy) in enumerate(NEAR):
-        copy = pltpu.make_async_remote_copy(
-            src_ref=sent.at[at(dx, dy)],
-            dst_ref=got.at[col],
-            send_sem=s1.at[i],
-            recv_sem=r1.at[i],
-            device_id=(row, at(dx, dy)),
-            device_id_type=MESH,
-        )
-        straight.append(copy)
+        target = at(dx, dy)
+        straight.append(remote(sent.at[target], got.at[col], s1.at[i], r1.at[i], target))
     for copy in straight[:4]:
         copy.start()
     onward = []
-    for leg, j, origin, target, first, count in legs:
+    for n, (leg, j, origin, target, first, size) in enumerate(legs):
         leg.wait_recv()
-        copy = pltpu.make_async_remote_copy(
-            src_ref=relay.at[j, pl.ds(0, count)],
-            dst_ref=got.at[origin, pl.ds(first, count)],
-            send_sem=s3.at[j],
-            recv_sem=r3.at[j],
-            device_id=(row, target),
-            device_id_type=MESH,
+        copy = remote(
+            relay.at[j], got.at[origin, pl.ds(first, size)], s3.at[j], r3.at[j], target
         )
         copy.start()
         onward.append(copy)
-    for copy in straight[4:]:
-        copy.start()
+        if n % 3 == 2 and 4 + n // 3 < len(straight):
+            straight[4 + n // 3].start()
+
     for copy in straight + onward:
         copy.wait()
     for leg, *_ in legs:
@@ -151,54 +176,69 @@
 
 
 def exchange(sent):
-    rows = sent.shape[1]
     return pl.pallas_call(
         exchange_kernel,
-        out_shape=jax.ShapeDtypeStruct(sent.shape, jnp.float32),
+        out_shape=jax.ShapeDtypeStruct((N_COL, 2 * SLOT, TILE), jnp.float32),
         in_specs=[ANY],
         out_specs=ANY,
-        scratch_shapes=[pltpu.VMEM((2 * len(FAR), cut(rows, 2)[1][1], TILE), jnp.float32), DMA]
+        scratch_shapes=[pltpu.VMEM((2 * len(FAR), SLOT, TILE), jnp.float32), DMA(())]
         + [DMA((len(NEAR),))] * 2
         + [DMA((2 * len(FAR),))] * 4,
         compiler_params=pltpu.CompilerParams(collective_id=1, has_side_effects=True),
         name="exchange",
-    )(sent)
-
-
-def assemble_kernel(target, front, got, out):
+    )(sent.reshape(N_COL, 2 * SLOT, TILE)).reshape(2 * N_COL, SLOT, TILE)
+
+
+def assemble_kernel(target, front, got, out, held, sems):
     band = pl.program_id(0)
+
+    def fetch(slot):
+        source = got.at[slot, pl.ds(0, TILE)]
+        return pltpu.make_async_copy(source, held.at[slot], sems.at[slot])
+
+    @pl.when(band == 0)
+    def _():
+        for slot in range(target.shape[0]):
+
+            @pl.when(target[slot] >= 0)
+            def _():
+                fetch(slot).start()
+
     out[...] = front[...]
     for slot in range(target.shape[0]):
         place = target[slot]
 
         @pl.when((place >= 0) & (place // 4 == band))
         def _():
+            fetch(slot).wait()
             lanes = pl.ds(pl.multiple_of(place % 4 * TILE, TILE), TILE)
-            out[:, lanes] += got[slot // CAP, pl.ds(slot % CAP * SLOT, TILE), :]
-
-
-def assemble(target, front, got):
+            out[:, lanes] += held[slot]
+
+
+def assemble(front, target, got):
     rows, cols = front.shape
+    slots = target.shape[0]
     return pl.pallas_call(
         assemble_kernel,
         out_shape=jax.ShapeDtypeStruct(front.shape, jnp.float32),
         grid_spec=pltpu.PrefetchScalarGridSpec(
             num_scalar_prefetch=1,
             grid=(rows // TILE,),
-            in_specs=[
-                pl.BlockSpec((TILE, cols), lambda i, t: (i, 0)),
-                pl.BlockSpec(got.shape, lambda i, t: (0, 0, 0), pipeline_mode=pl.Buffered(1)),
-            ],
+            in_specs=[pl.BlockSpec((TILE, cols), lambda i, t: (i, 0))] + [ANY],
             out_specs=pl.BlockSpec((TILE, cols), lambda i, t: (i, 0)),
+            scratch_shapes=[pltpu.VMEM((slots, TILE, TILE), jnp.float32), DMA((slots,))],
         ),
         name="assemble",
     )(target, front, got)
 
 
-PIECE = 32
-PIECES = 16
+PIECE = 16
+PIECES = 32
 BAND = 16
-CORNER_AT = 10
+BANDS = 16
+HOP = 3
+CORNER_AT = 23
+CORNER_HOP = 6
 
 
 def spanning_trees():
@@ -297,7 +337,7 @@
 
     def step(now, carry):
         for tree in range(4):
-            piece = now - level[tree] - 1
+            piece = now - HOP * level[tree] - 1
 
             @pl.when((piece == -1) & upper)
             def _():
@@ -334,7 +374,7 @@
 
         for half in range(2):
             hops = way[half]
-            piece = now - hops
+            piece = now - HOP * hops
 
             def band_copy(source, which):
                 target = band_piece(band, half, piece)
@@ -342,7 +382,7 @@
                     return remote(source, target, us.at[half], ur.at[half, piece], along[half])
                 return remote(source, target, qs.at[half], qr.at[half], partner)
 
-            @pl.when(leads & (piece >= 0) & (piece < PIECES))
+            @pl.when(leads & (piece >= 0) & (piece < BANDS))
             def _():
                 @pl.when(hops == 0)
                 def _():
@@ -368,7 +408,7 @@
 
                 remote(source, corner_half(half), ws.at[half], wr.at[half], partner).start()
 
-            @pl.when(leads & (now == CORNER_AT + 3 * hops))
+            @pl.when(leads & (now == CORNER_AT + CORNER_HOP * hops))
             def _():
                 @pl.when(upper & root)
                 def _():
@@ -392,7 +432,7 @@
 
         return carry
 
-    lax.fori_loop(0, PIECES + 6, step, 0)
+    lax.fori_loop(0, PIECES + 1 + 5 * HOP, step, 0)
 
     whole = block.at[pl.ds(0, PIECE * PIECES)]
     for tree in range(4):
@@ -455,7 +495,7 @@
             DMA((4, 4)),
             DMA((4,)),
             DMA((2,)),
-            DMA((2, PIECES)),
+            DMA((2, BANDS)),
         ]
         + [DMA((2,))] * 6,
         compiler_params=pltpu.CompilerParams(collective_id=2, has_side_effects=True),
@@ -464,12 +504,14 @@
 
 
 def update_kernel(
-    front, block, band, corner, top, side, inverse, out, up_high, up_low, small_high, small_low
+    front, block, band, corner, top, side, inverse, out,
+    up_high, up_low, near_high, near_low, mix_high, mix_low,
 ):
     step = pl.program_id(0)
     row = lax.axis_index("row")
     root = lax.axis_index("col") == 0
     upper = row == 0
+    number = row * pl.num_programs(0) + step
 
     @pl.when(step == 0)
     def _():
@@ -477,38 +519,54 @@
         right = jnp.where(upper & root, top[:TILE, TILE : 2 * TILE], corner[:TILE])
         below = jnp.where(root, top[TILE:, :TILE], side[...])
         below = jnp.where(upper, below, corner[TILE:])
-        for place, value in enumerate((inverse[0], inverse[1], right)):
-            small_high[place], small_low[place] = halves(value)
-        first = band_now[:TILE]
-        first_parts = halves(first)
-        ratio = product3(halves(below), (small_high[0], small_low[0]))
-        second = band_now[TILE:] - product3(halves(ratio), first_parts)
-        up_high[:TILE], up_low[:TILE] = first_parts
-        up_high[TILE:], up_low[TILE:] = halves(second)
-
-    current = front[...]
-    columns = jnp.where(root, current[:, : 2 * TILE], block[...])
-    lower_0 = product3(halves(columns[:, :TILE]), (small_high[0], small_low[0]))
-    lower_0_parts = halves(lower_0)
-    rest = columns[:, TILE:] - product3(lower_0_parts, (small_high[2], small_low[2]))
-    lower_1 = product3(halves(rest), (small_high[1], small_low[1]))
-    number = row * (N_ROW * TILE // TILE) + step
-    live_0 = number >= 1
-    live_1 = number >= 2
-    both = jnp.concatenate(
-        [jnp.where(live_0, lower_0, 0.0), jnp.where(live_1, lower_1, 0.0)], axis=1
-    )
-    high, low = halves(both)
-    update = product3((high, low), (up_high[...], up_low[...]))
-    out[...] = current - update
-
-    @pl.when(root & live_0)
+        inverse_0, inverse_1 = halves(inverse[0]), halves(inverse[1])
+        first = halves(band_now[:TILE])
+        ahead = product3(inverse_0, first)
+        cross = product3(halves(below), halves(ahead))
+        second = halves(band_now[TILE:] - cross)
+        mixed = product3(halves(right), inverse_1)
+        mixed = product3(inverse_0, halves(mixed))
+        mix = halves(mixed)
+        near_high[...], near_low[...] = halves(ahead)
+        up_high[:TILE], up_low[:TILE] = halves(ahead - product3(mix, second))
+        up_high[TILE:], up_low[TILE:] = halves(product3(inverse_1, second))
+        for place, parts in enumerate((inverse_0, inverse_1, mix)):
+            mix_high[place], mix_low[place] = parts
+
+    @pl.when(number == 0)
     def _():
-        out[:, :TILE] = lower_0
-
-    @pl.when(root & live_1)
+        out[...] = front[...]
+
+    @pl.when((number > 0) & jnp.logical_not(root))
     def _():
-        out[:, TILE : 2 * TILE] = lower_1
+        high, low = halves(block[...])
+
+        @pl.when(number > 1)
+        def _():
+            out[...] = front[...] - product3((high, low), (up_high[...], up_low[...]))
+
+        @pl.when(number == 1)
+        def _():
+            left = high[:, :TILE], low[:, :TILE]
+            out[...] = front[...] - product3(left, (near_high[...], near_low[...]))
+
+    @pl.when((number > 0) & root)
+    def _():
+        high, low = halves(front[:, : 2 * TILE])
+        left, right = (high[:, :TILE], low[:, :TILE]), (high[:, TILE:], low[:, TILE:])
+        out[:, :TILE] = product3(left, (mix_high[0], mix_low[0]))
+
+        @pl.when(number > 1)
+        def _():
+            lower = product3(right, (mix_high[1], mix_low[1]))
+            out[:, TILE : 2 * TILE] = lower - product3(left, (mix_high[2], mix_low[2]))
+            parts = up_high[:, 2 * TILE :], up_low[:, 2 * TILE :]
+            out[:, 2 * TILE :] = front[:, 2 * TILE :] - product3((high, low), parts)
+
+        @pl.when(number == 1)
+        def _():
+            parts = near_high[:, TILE:], near_low[:, TILE:]
+            out[:, TILE:] = front[:, TILE:] - product3(left, parts)
 
 
 def update(front, block, band, corner, inverse):
@@ -529,6 +587,7 @@
         ],
         out_specs=pl.BlockSpec((TILE, cols), lambda i: (i, 0)),
         scratch_shapes=[pltpu.VMEM((2 * TILE, cols), jnp.bfloat16)] * 2
+        + [pltpu.VMEM((TILE, cols), jnp.bfloat16)] * 2
         + [pltpu.VMEM((3, TILE, TILE), jnp.bfloat16)] * 2,
         name="update",
     )(front, block, band, corner, front, block, inverse)
@@ -538,24 +597,16 @@
     front_matrix, child_tiles, target_column, target_tile, row_map, col_map, pivot_inverse
 ):
     count = child_tiles.shape[2]
-    targets = target_column.reshape(count)
-    numbers = jnp.arange(count, dtype=jnp.int32)
-    earlier = (targets[:, None] == targets[None, :]) & (numbers[None, :] < numbers[:, None])
-    placed = targets * CAP + jnp.sum(earlier.astype(jnp.int32), axis=1)
-    slots = jnp.arange(N_COL * CAP, dtype=jnp.int32)
-    match = placed[None, :] == slots[:, None]
-    source = jnp.sum(jnp.where(match, numbers[None, :], 0), axis=1)
-    mark = jnp.sum(jnp.where(match, target_tile.reshape(1, count) + 1, 0), axis=1) - 1
-    sent = permute(
-        source,
-        mark,
+    rows = front_matrix.shape[0]
+    routed = (
+        target_column.reshape(count),
+        target_tile.reshape(count),
         child_tiles.reshape(count, TILE, TILE),
         row_map.reshape(count, TILE),
         col_map.reshape(count, TILE),
     )
-    got = exchange(sent.reshape(N_COL, CAP * SLOT, TILE))
-    target = got.reshape(N_COL * CAP, SLOT, TILE)[:, TILE, 0].astype(jnp.int32)
-    front = assemble(target, front_matrix, got)
+    got = exchange(permute(*routed))
+    front = assemble(front_matrix, got[:, TILE, 0].astype(jnp.int32), got)
     block, band, corner = share_panels(front)
     return update(front, block, band, corner, pivot_inverse)
 

time: 276 us -> 223 us (0.81)
  Pallas kernels: 268 us -> 220 us
  local copies, waits for them, and re-layouts: 3.65 us -> 0 us
    pallas_call x1, Pallas kernels: 27.3 us -> 10.4 us  [permute(): pl.pallas_call(permute_kernel, out_shape=jax.ShapeDtypeStruct((slots, SLO...]
    pallas_call x1, Pallas kernels: 82.2 us -> 67 us  [share_panels(): pl.pallas_call(panel_kernel, out_shape=(jax.ShapeDtypeStruct((rows, 2 * T...]
    pallas_call x1, Pallas kernels: 122 us -> 111 us  [exchange(): pl.pallas_call(exchange_kernel, out_shape=jax.ShapeDtypeStruct((N_COL, 2...]
    pallas_call x1, Pallas kernels: 22.5 us -> 17.5 us  [update(): pl.pallas_call(update_kernel, out_shape=jax.ShapeDtypeStruct(front.shape,...]
where the time goes in v2:
time: 223 us; the launch traced here: 222 us
  Pallas kernels  220 us (99%)
    pallas_call x1, Pallas kernels, exchange(): pl.pallas_call(exchange_kernel, out_shape=jax.ShapeDtypeStruct((N_COL, 2...  111 us
    pallas_call x1, Pallas kernels, share_panels(): pl.pallas_call(panel_kernel, out_shape=(jax.ShapeDtypeStruct((rows, 2 * T...  67 us
    pallas_call x1, Pallas kernels, update(): pl.pallas_call(update_kernel, out_shape=jax.ShapeDtypeStruct(front.shape,...  17.5 us
    pallas_call x1, Pallas kernels, assemble(): pl.pallas_call(assemble_kernel, out_shape=jax.ShapeDtypeStruct(front.shap...  14.1 us
    pallas_call x1, Pallas kernels, permute(): pl.pallas_call(permute_kernel, out_shape=jax.ShapeDtypeStruct((slots, SLO...  10.4 us

profile of v2, /device:TPU:12, one launch (start us, length us, event | category | flops | bytes accessed | tf_op | source)
XLA Modules:
  0.0 222.2 jit_solution(15218363473730275950)
XLA Ops:
  0.0 10.4 %permute.1 = f32[32,264,256]{2,1,0:T(8,128)} custom-call(s32[16]{0:T(128)} %bitcast.13, s32[16]{0:T(128)} %bitcast.14, f32[16,256,256]{2,1,0:T(8,128)} %bitcast.10, s32[16,256]{1,0:T(8,128)} %bitcast.11, s32[16,256]{1,0:T(8,128)} %bitcast.12), custom_call_target="tpu_custom_call" | custom-call | tf_op jit(solution)/shard_map/permute/pallas_call | solution.py:87
  10.4 111.0 %exchange.1 = f32[16,528,256]{2,1,0:T(8,128)} custom-call(f32[16,528,256]{2,1,0:T(8,128)} %bitcast.9), custom_call_target="tpu_custom_call" | custom-call | tf_op jit(solution)/shard_map/exchange/pallas_call | solution.py:179
  121.4 2.1 fusion.target
  123.5 14.1 %assemble.1.front.top = f32[2048,1024]{1,0:T(8,128)} custom-call(s32[32]{0:T(128)} %fusion.target, f32[2048,1024]{1,0:T(8,128)} %front.1, f32[32,264,256]{2,1,0:T(8,128)} %bitcast.8), custom_call_target="tpu_custom_call" | custom-call | tf_op jit(solution)/shard_map/assemble/pallas_call | solution.py:221
  137.6 67.0 %share_panels.1 = (f32[2048,512]{1,0:T(8,128)}, f32[512,1024]{1,0:T(8,128)}, f32[512,256]{1,0:T(8,128)}) custom-call(f32[2048,1024]{1,0:T(8,128)} %assemble.1.front.top), custom_call_target="tpu_custom_call" | custom-call | tf_op jit(solution)/shard_map/share_panels/pallas_call | solution.py:483
  204.6 17.5 %update.1 = f32[2048,1024]{1,0:T(8,128)} custom-call(f32[2048,1024]{1,0:T(8,128)} %assemble.1.front.top, f32[2048,512]{1,0:T(8,128)} %get-tuple-element.8.block.side, f32[512,1024]{1,0:T(8,128)} %get-tuple-element.9.band, f32[512,256]{1,0:T(8,128)} %get-tuple-element.10.corner, f32[2048,1024]{1,0:T(8,128)} %assemble.1.front.top, ...), custom_call_target="tpu_custom_call" | custom-call | tf_op jit(solution)/shard_map/update/pallas_call | solution.py:575

commit v3 on v2

--- a/solution.py
+++ b/solution.py
@@ -232,13 +232,13 @@
     )(target, front, got)
 
 
-PIECE = 16
-PIECES = 32
+PIECE = 32
+PIECES = 16
 BAND = 16
 BANDS = 16
 HOP = 3
-CORNER_AT = 23
-CORNER_HOP = 6
+CORNER_AT = 19
+CORNER_HOP = 4
 
 
 def spanning_trees():

time: 223 us -> 213 us (0.955)
  the two profiles are of different devices: /device:TPU:12 before, /device:TPU:35 now
where the time goes in v3:
time: 213 us
  Pallas kernels  211 us (99%)
    pallas_call x1, Pallas kernels, exchange(): pl.pallas_call(exchange_kernel, out_shape=jax.ShapeDtypeStruct((N_COL, 2...  113 us
    pallas_call x1, Pallas kernels, share_panels(): pl.pallas_call(panel_kernel, out_shape=(jax.ShapeDtypeStruct((rows, 2 * T...  55.5 us
    pallas_call x1, Pallas kernels, update(): pl.pallas_call(update_kernel, out_shape=jax.ShapeDtypeStruct(front.shape,...  18.4 us
    pallas_call x1, Pallas kernels, assemble(): pl.pallas_call(assemble_kernel, out_shape=jax.ShapeDtypeStruct(front.shap...  12.9 us
    pallas_call x1, Pallas kernels, permute(): pl.pallas_call(permute_kernel, out_shape=jax.ShapeDtypeStruct((slots, SLO...  10.5 us

profile of v3, /device:TPU:35, one launch (start us, length us, event | category | flops | bytes accessed | tf_op | source)
XLA Modules:
  0.0 212.8 jit_solution(4227816585716954745)
XLA Ops:
  0.0 10.5 %permute.1 = f32[32,264,256]{2,1,0:T(8,128)} custom-call(s32[16]{0:T(128)} %bitcast.13, s32[16]{0:T(128)} %bitcast.14, f32[16,256,256]{2,1,0:T(8,128)} %bitcast.10, s32[16,256]{1,0:T(8,128)} %bitcast.11, s32[16,256]{1,0:T(8,128)} %bitcast.12), custom_call_target="tpu_custom_call" | custom-call | tf_op jit(solution)/shard_map/permute/pallas_call | solution.py:87
  10.5 113.4 %exchange.1 = f32[16,528,256]{2,1,0:T(8,128)} custom-call(f32[16,528,256]{2,1,0:T(8,128)} %bitcast.9), custom_call_target="tpu_custom_call" | custom-call | tf_op jit(solution)/shard_map/exchange/pallas_call | solution.py:179
  123.9 2.1 fusion.target
  126.0 12.9 %assemble.1.front.top = f32[2048,1024]{1,0:T(8,128)} custom-call(s32[32]{0:T(128)} %fusion.target, f32[2048,1024]{1,0:T(8,128)} %front.1, f32[32,264,256]{2,1,0:T(8,128)} %bitcast.8), custom_call_target="tpu_custom_call" | custom-call | tf_op jit(solution)/shard_map/assemble/pallas_call | solution.py:221
  138.9 55.5 %share_panels.1 = (f32[2048,512]{1,0:T(8,128)}, f32[512,1024]{1,0:T(8,128)}, f32[512,256]{1,0:T(8,128)}) custom-call(f32[2048,1024]{1,0:T(8,128)} %assemble.1.front.top), custom_call_target="tpu_custom_call" | custom-call | tf_op jit(solution)/shard_map/share_panels/pallas_call | solution.py:483
  194.4 18.4 %update.1 = f32[2048,1024]{1,0:T(8,128)} custom-call(f32[2048,1024]{1,0:T(8,128)} %assemble.1.front.top, f32[2048,512]{1,0:T(8,128)} %get-tuple-element.8.block.side, f32[512,1024]{1,0:T(8,128)} %get-tuple-element.9.band, f32[512,256]{1,0:T(8,128)} %get-tuple-element.10.corner, f32[2048,1024]{1,0:T(8,128)} %assemble.1.front.top, ...), custom_call_target="tpu_custom_call" | custom-call | tf_op jit(solution)/shard_map/update/pallas_call | solution.py:575
